TPU v7x, 512 devices: a whole 4x8x8 slice. The times are simulated.
512 devices in a mesh: row: 16 (over y, core), col: 32 (over z, x).
Axes of the slice: x: 4, y: 8, z: 8, core: 2. Of those that a mesh axis runs over, the one named last changes fastest.
Arguments:
- start_block: float32 [4, 65536], P(None, ('row', 'col')), may hold values from -6 to 6
- matrix_tiles: float32 [4096, 256, 256], P(('row', 'col')), may hold values from -0.125 to 0.125
- tile_rows: int32 [4096], P(('row', 'col')), may hold values from 0 to 255, as said below
- tile_cols: int32 [4096], P(('row', 'col')), may hold values from 0 to 255, as said below
- tile_counts: int32 [512], P(('row', 'col')), may hold values from 1 to 8
Outputs:
- next_basis: float32 [4, 65536], P(None, ('row', 'col'))
- next_residual: float32 [4, 65536], P(None, ('row', 'col'))
- coefficients: float32 [3, 4, 4], replicated
Inputs may be any that keep to these rules, and one draw needn't show every extreme that they name: `tile_rows`: A slot of device d holds a tile whose row lies among the 16 tile rows (d // 32) * 16 onward and whose column lies among the 8 tile columns (d % 32) * 8 onward; its row I and column J satisfy I == J, or I < J with I + J odd, or I > J with I + J even; the slots of one device hold distinct tiles. `tile_cols`: paired with tile_rows slot by slot, as described there.
All inputs are finite; a program needn't handle non-finite values.
Results may differ from a plain program's by a relative error of at most 0.000098.
Values sent between devices are 32-bit elements; how exact they have to be, the bound alone decides.
A program may use at most 64 MiB of HBM per device.

v0:
```python
import jax
import jax.numpy as jnp
from jax import lax
from jax.sharding import PartitionSpec as P

epsilon = 1e-06


def local_dots(first, second):
    return jnp.dot(first, second.T, precision=lax.Precision.HIGHEST)


def factorize(gram_matrix):
    eye_matrix = jnp.eye(gram_matrix.shape[0], dtype=gram_matrix.dtype)
    return jnp.linalg.cholesky(gram_matrix + epsilon * eye_matrix)


def local_products(current, matrix_tiles, tile_rows, tile_cols, tile_counts):
    spread_ratio = lax.axis_size("col") // lax.axis_size("row")
    row_index = lax.axis_index("row")
    column_index = lax.axis_index("col")
    tile_width = matrix_tiles.shape[1]
    column_length = current.shape[1] // spread_ratio
    whole = lax.all_gather(current, "row", axis=1, tiled=True)
    column_part = lax.dynamic_slice_in_dim(whole, column_index * column_length, column_length, 1)
    row_base = row_index * (current.shape[1] // tile_width)
    column_base = column_index * (column_length // tile_width)

    def add_tile(slot_index, partials):
        forward, backward = partials
        current_tile = lax.dynamic_index_in_dim(matrix_tiles, slot_index, 0, keepdims=False)
        row_start = (tile_rows[slot_index] - row_base) * tile_width
        column_start = (tile_cols[slot_index] - column_base) * tile_width
        from_column = lax.dynamic_slice_in_dim(column_part, column_start, tile_width, 1)
        from_row = lax.dynamic_slice_in_dim(current, row_start, tile_width, 1)
        out_forward = lax.dot_general(
            from_column, current_tile, (((1,), (1,)), ((), ())), precision=lax.Precision.HIGHEST
        )
        out_backward = jnp.dot(from_row, current_tile, precision=lax.Precision.HIGHEST)
        forward = lax.dynamic_update_slice_in_dim(
            forward,
            lax.dynamic_slice_in_dim(forward, row_start, tile_width, 1) + out_forward,
            row_start,
            1,
        )
        backward = lax.dynamic_update_slice_in_dim(
            backward,
            lax.dynamic_slice_in_dim(backward, column_start, tile_width, 1) + out_backward,
            column_start,
            1,
        )
        return (forward, backward)

    start_state = (
        jnp.zeros(current.shape, jnp.float32),
        jnp.zeros((current.shape[0], column_length), jnp.float32),
    )
    forward, backward = lax.fori_loop(0, tile_counts[0], add_tile, start_state)
    column_total = lax.psum(backward, "row")
    owner_flag = jnp.where(row_index == column_index // spread_ratio, 1.0, 0.0).astype(jnp.float32)
    placed = lax.dynamic_update_slice_in_dim(
        jnp.zeros_like(forward),
        column_total * owner_flag,
        column_index % spread_ratio * column_length,
        1,
    )
    return forward + placed


def body(start_block, matrix_tiles, tile_rows, tile_cols, tile_counts):
    rows_here = lax.all_gather(start_block, "col", axis=1, tiled=True)
    order_total = rows_here.shape[1] * lax.axis_size("row")
    start_gram = lax.psum(local_dots(rows_here, rows_here), "row") / order_total
    start_factor = factorize(start_gram)
    first_basis = lax.linalg.triangular_solve(start_factor, rows_here, left_side=True, lower=True)
    image = lax.psum(
        local_products(first_basis, matrix_tiles, tile_rows, tile_cols, tile_counts), "col"
    )
    first_diag = lax.psum(local_dots(first_basis, image), "row") / order_total
    first_rest = image - jnp.dot(first_diag.T, first_basis, precision=lax.Precision.HIGHEST)
    rest_gram = lax.psum(local_dots(first_rest, first_rest), "row") / order_total
    first_factor = factorize(rest_gram)
    next_basis = lax.linalg.triangular_solve(first_factor, first_rest, left_side=True, lower=True)
    second_terms = local_products(next_basis, matrix_tiles, tile_rows, tile_cols, tile_counts)
    share = rows_here.shape[1] // lax.axis_size("col")
    offset = lax.axis_index("col") * share
    basis_out = lax.dynamic_slice_in_dim(next_basis, offset, share, 1)
    first_share = lax.dynamic_slice_in_dim(first_basis, offset, share, 1)
    second_image = lax.psum(second_terms, "col")
    second_diag = lax.psum(local_dots(next_basis, second_image), "row") / order_total
    image_share = lax.dynamic_slice_in_dim(second_image, offset, share, 1)
    residual_out = (
        image_share
        - jnp.dot(second_diag.T, basis_out, precision=lax.Precision.HIGHEST)
        - jnp.dot(first_factor.T, first_share, precision=lax.Precision.HIGHEST)
    )
    coefficients = jnp.stack([first_diag, second_diag, first_factor])
    return (basis_out, residual_out, coefficients)


def solution(mesh):
    return jax.shard_map(
        body,
        mesh=mesh,
        in_specs=(
            P(None, ("row", "col")),
            P(("row", "col"), None, None),
            P(("row", "col")),
            P(("row", "col")),
            P(("row", "col")),
        ),
        out_specs=(P(None, ("row", "col")), P(None, ("row", "col")), P()),
        check_vma=False,
    )
```

profile of v0, /device:TPU:1, one launch (start us, length us, event | category | flops | bytes accessed | tf_op | source)
XLA Modules:
  0.0 770.8 jit_solution(6399266472147339740)
XLA Ops:
  7.2 43.6 %all_gather.9 = f32[4,4096]{1,0:T(4,128)S(1)} all-gather(f32[4,128]{1,0:T(4,128)} %param.12), channel_id=1, replica_groups=mesh['row'=16,'col'=32] {'col'}, dimensions={1}, use_global_device_ids=true | all-gather | bytes 67584 | tf_op jit(solution)/shard_map/all_gather | solution.py:71
  51.1 36.5 %psum.56 = f32[4,4]{0,1:T(4,128)S(1)} all-reduce(f32[4,4]{0,1:T(4,128)S(1)} %fusion.34), channel_id=1, replica_groups=mesh['row'=16,'col'=32] {'row'}, use_global_device_ids=true, to_apply=%region_0.0 | all-reduce | flops 16 | bytes 128 | tf_op jit(solution)/shard_map/psum | solution.py:73
  90.9 37.3 %all-gather.3.cloned.1.call-done = f32[4,65536]{1,0:T(4,128)} async-done(((f32[4,4096]{1,0:T(4,128)}), f32[4,65536]{1,0:T(4,128)}) %all-gather.3.cloned.1.call-update) | async-done | bytes 1048592 | tf_op jit(solution)/shard_map/all_gather | solution.py:24
  128.9 29.4 %while.32 = (s32[]{:T(128)}, f32[4,4096]{1,0:T(4,128)S(1)}, f32[4,2048]{1,0:T(4,128)S(1)}, s32[]{:T(128)}, s32[8]{0:T(128)}, /*index=5*/s32[]{:T(128)}, s32[8]{0...) while((s32[]{:T(128)}, f32[4,4096]{1,0:T(4,128)S(1)}, ...), condition=%wide.region_4.7_spmd, body=%wide.region_3.0_spmd.sunk | while | flops 6293519 | bytes 549219 | solution.py:58
  131.6 1.3 dynamic_slice.121
  138.8 1.3 dynamic_slice.121
  146.0 1.3 dynamic_slice.121
  151.2 1.3 dynamic_slice.122
  153.2 1.3 dynamic_slice.121
  158.3 71.2 %psum.57 = f32[4,2048]{1,0:T(4,128)S(1)} all-reduce(f32[4,2048]{1,0:T(4,128)S(1)} %get-tuple-element.124), channel_id=1, replica_groups=mesh['row'=16,'col'=32] {'row'}, use_global_device_ids=true, to_apply=%region_5.8 | all-reduce | flops 8192 | bytes 65536 | tf_op jit(solution)/shard_map/psum | solution.py:59
  230.3 151.3 %all-reduce.3.cloned.1.call-done = f32[4,4096]{1,0:T(4,128)} async-done(((f32[4,4096]{1,0:T(4,128)}), f32[4,4096]{1,0:T(4,128)}) %all-reduce.3.cloned.1.call-update) | async-done | bytes 65552 | tf_op jit(solution)/shard_map/psum | solution.py:76
  382.8 27.9 %psum.59 = f32[4,4]{0,1:T(4,128)S(1)} all-reduce(f32[4,4]{0,1:T(4,128)S(1)} %fusion.35), channel_id=1, replica_groups=mesh['row'=16,'col'=32] {'row'}, use_global_device_ids=true, to_apply=%region_7.10 | all-reduce | flops 16 | bytes 128 | tf_op jit(solution)/shard_map/psum | solution.py:79
  412.2 23.6 %psum.60 = f32[4,4]{0,1:T(4,128)S(1)} all-reduce(f32[4,4]{0,1:T(4,128)S(1)} %fusion.36), channel_id=1, replica_groups=mesh['row'=16,'col'=32] {'row'}, use_global_device_ids=true, to_apply=%region_8.11 | all-reduce | flops 16 | bytes 128 | tf_op jit(solution)/shard_map/psum | solution.py:81
  439.1 38.9 %all-gather.5.cloned.1.call-done = f32[4,65536]{1,0:T(4,128)} async-done(((f32[4,4096]{1,0:T(4,128)}), f32[4,65536]{1,0:T(4,128)}) %all-gather.5.cloned.1.call-update) | async-done | bytes 1048592 | tf_op jit(solution)/shard_map/all_gather | solution.py:24
  478.8 29.4 %while.33 = (s32[]{:T(128)}, f32[4,4096]{1,0:T(4,128)S(1)}, f32[4,2048]{1,0:T(4,128)S(1)}, s32[]{:T(128)}, s32[8]{0:T(128)}, /*index=5*/s32[]{:T(128)}, s32[8]{0...) while((s32[]{:T(128)}, f32[4,4096]{1,0:T(4,128)S(1)}, ...), condition=%wide.region_10.13_spmd, body=%wide.region_9.12_spmd.sunk | while | flops 6293519 | bytes 549219 | solution.py:58
  479.5 1.3 dynamic_slice.130
  481.5 1.3 dynamic_slice.129
  488.7 1.3 dynamic_slice.129
  495.9 1.3 dynamic_slice.129
  503.1 1.3 dynamic_slice.129
  508.3 71.2 %psum.61 = f32[4,2048]{1,0:T(4,128)S(1)} all-reduce(f32[4,2048]{1,0:T(4,128)S(1)} %get-tuple-element.126), channel_id=1, replica_groups=mesh['row'=16,'col'=32] {'row'}, use_global_device_ids=true, to_apply=%region_11.14 | all-reduce | flops 8192 | bytes 65536 | tf_op jit(solution)/shard_map/psum | solution.py:59
  580.8 150.7 %all-reduce.5.cloned.1.call-done = f32[4,4096]{1,0:T(4,128)} async-done(((f32[4,4096]{1,0:T(4,128)}), f32[4,4096]{1,0:T(4,128)}) %all-reduce.5.cloned.1.call-update) | async-done | bytes 65552 | tf_op jit(solution)/shard_map/psum | solution.py:89
  732.7 27.9 %psum.63 = f32[4,4]{0,1:T(4,128)S(1)} all-reduce(f32[4,4]{0,1:T(4,128)S(1)} %fusion.37), channel_id=1, replica_groups=mesh['row'=16,'col'=32] {'row'}, use_global_device_ids=true, to_apply=%region_13.16 | all-reduce | flops 16 | bytes 128 | tf_op jit(solution)/shard_map/psum | solution.py:90
  761.6 2.1 convolution_subtract_fusion.1
  (74 shorter events, 43.2 us)
Async XLA Ops:
  7.2 121.0 %all-gather.3.cloned.1.call-start = ((), (), s32[]{:S(2)}) async-start(), calls=%async_computation | async-start | bytes 1114112 | tf_op jit(solution)/shard_map/all_gather | solution.py:24
  90.8 290.8 %all-reduce.3.cloned.1.call-start = ((), (), s32[]{:S(2)}) async-start(), calls=%async_computation.1 | async-start | bytes 131072 | tf_op jit(solution)/shard_map/psum | solution.py:76
  229.6 0.6 copy-start.1
  230.2 247.8 %all-gather.5.cloned.1.call-start = ((), (), s32[]{:S(2)}) async-start(), calls=%async_computation.2 | async-start | bytes 1114112 | tf_op jit(solution)/shard_map/all_gather | solution.py:24
  438.9 292.5 %all-reduce.5.cloned.1.call-start = ((), (), s32[]{:S(2)}) async-start(), calls=%async_computation.3 | async-start | bytes 131072 | tf_op jit(solution)/shard_map/psum | solution.py:89
  579.5 0.6 copy-start
  580.8 183.4 %copy-start.2 = (f32[4,128]{1,0:T(4,128)}, f32[4,128]{1,0:T(4,128)S(1)}, u32[]{:S(2)}) copy-start(f32[4,128]{1,0:T(4,128)S(1)} %constant_dynamic-slice_fusion.2) | copy-start | bytes 6148
Sparse Core Ops, SparseCore 0:
  90.9 37.1 all-gather.2
  230.4 151.1 all-reduce.2
  439.1 38.9 all-gather.4
  580.3 151.1 all-reduce.4
where the time goes:
time: 773 us; the launch traced here: 771 us
  waiting for transfers between devices  378 us (49%)
  blocking collectives  302 us (39%)
  matrix products  28.5 us (4%)
  local copies, waits for them, and re-layouts  25 us (3%)
  loops' own time  18.2 us (2%)
  between operations  13.9 us (2%)
    psum x1, waiting for transfers between devices, body(): lax.psum(local_products(first_basis, matrix_tiles, tile_rows, tile_cols,...  151 us
    psum x1, waiting for transfers between devices, body(): second_image = lax.psum(second_terms, 'col')  151 us
    psum x2, blocking collectives, local_products(): column_total = lax.psum(backward, 'row')  142 us
    all_gather x2, waiting for transfers between devices, local_products(): whole = lax.all_gather(current, 'row', axis=1, tiled=True)  76.2 us
    all_gather x1, blocking collectives, body(): rows_here = lax.all_gather(start_block, 'col', axis=1, tiled=True)  43.6 us
    psum x1, blocking collectives, body(): start_gram = lax.psum(local_dots(rows_here, rows_here), 'row') / order_total  36.5 us
    psum x1, blocking collectives, body(): first_diag = lax.psum(local_dots(first_basis, image), 'row') / order_total  27.9 us
    psum x1, blocking collectives, body(): lax.psum(local_dots(next_basis, second_image), 'row') / order_total  27.9 us
  transfers between devices with their start and end apart: 4, of which 4 were waited for; matrix products, arithmetic and copies ran while one was open for 0% of the time, Pallas kernels for 0%

commit v1 on v0

v1 whole, which is shorter than its diff:
```python
import jax
import jax.numpy as jnp
from jax import lax
from jax.experimental import pallas as pl
from jax.experimental.pallas import tpu as pltpu
from jax.sharding import PartitionSpec as P

MESH = pl.DeviceIdType.MESH
epsilon = 1e-06
VEC, TILE, SLOTS, LANES = 4, 256, 8, 128
ROWS, COLS = 16, 32
HALF = COLS // 2
ROW_TILES, COL_TILES = 16, 8
ORDER = ROWS * COLS * LANES

ROW0, COL0, FWD0, BWD0, ROW1, COL1, FWD1, BWD1, PLANE0, LINE0, PLANE1, LINE1, PLANE2, LINE2 = range(14)


def iota(shape, axis):
    return lax.broadcasted_iota(jnp.int32, shape, axis)


def apply(matrix, block):
    return sum(matrix[:, j : j + 1] * block[j : j + 1, :] for j in range(VEC))


def rotated(block, offset):
    if offset == 0:
        return block
    keep = iota((8, LANES), 0) % VEC + offset < VEC
    return jnp.where(keep, pltpu.roll(block, 8 - offset, 0), pltpu.roll(block, VEC - offset, 0))


def gram_row(products):
    total = jnp.zeros((8, LANES), jnp.float32)
    lane, row = iota((8, LANES), 1), iota((8, LANES), 0)
    for offset, product in enumerate(products):
        summed = jnp.sum(product, axis=1, keepdims=True)
        total = jnp.where(lane == VEC * offset + row % VEC, summed, total)
    return jnp.sum(total, axis=0, keepdims=True)


def entry(gram, base, i, j):
    lane = base + VEC * ((j - i) % VEC) + i
    return gram[:, lane : lane + 1]


def assemble(entries):
    lane, row = iota((VEC, LANES), 1), iota((VEC, LANES), 0)
    total = jnp.zeros((VEC, LANES), jnp.float32)
    for (i, j), value in entries.items():
        total = jnp.where((row == i) & (lane == j), value, total)
    return total


def factorize(gram, base):
    a = {(i, j): entry(gram, base, i, j) * (1.0 / ORDER) for i in range(VEC) for j in range(i + 1)}
    low, inv = {}, {}
    for j in range(VEC):
        pivot = a[j, j] + epsilon
        for k in range(j):
            pivot = pivot - low[j, k] * low[j, k]
        low[j, j] = jnp.sqrt(pivot)
        inv[j, j] = 1.0 / low[j, j]
        for i in range(j + 1, VEC):
            rest = a[i, j]
            for k in range(j):
                rest = rest - low[i, k] * low[j, k]
            low[i, j] = rest * inv[j, j]
    for j in range(VEC):
        for i in range(j + 1, VEC):
            rest = low[i, j] * inv[j, j]
            for k in range(j + 1, i):
                rest = rest + low[i, k] * inv[k, j]
            inv[i, j] = -rest * inv[i, i]
    flip = lambda entries: {(j, i): value for (i, j), value in entries.items()}
    return assemble(low), assemble(inv), assemble(flip(inv)), assemble(flip(low))


def projected(gram, inverse, inverse_t):
    entries = {}
    for i in range(VEC):
        for j in range(i + 1):
            value = (entry(gram, 0, i, j) + entry(gram, 0, j, i)) * (1.0 / ORDER)
            entries[i, j] = value
            entries[j, i] = value
    return apply(apply(inverse, assemble(entries)), inverse_t)


def split(block, row):
    high = block.astype(jnp.bfloat16).astype(jnp.float32)
    return jnp.where(row < VEC, high, block - high)


def twice(block):
    return jnp.concatenate([block, block], axis=0)


def kernel(
    x_ref, tiles_ref, rows_ref, cols_ref, count_ref,
    basis_ref, resid_ref, coef_ref,
    raw, t_high, t_low, own, xr, xc, row_parts, col_parts, row_packed,
    fp, bp, fr, br, gsrc, gp, gy, tsem, ssem, rsem,
):
    r, c = lax.axis_index("row"), lax.axis_index("col")
    group = 2 * r + c // HALF
    owner_row, owner_col = c // 2, HALF * (c % 2)
    lane_at = c % HALF
    eight = iota((8, LANES), 0)

    def send(src, dst, exchange, row, col):
        pltpu.make_async_remote_copy(
            src_ref=src, dst_ref=dst, send_sem=ssem.at[exchange], recv_sem=rsem.at[exchange],
            device_id=(row, col), device_id_type=MESH,
        ).start()

    def wait(sem, ref):
        pltpu.make_async_copy(ref, ref, sem).wait()

    def loop(first, last, body):
        def step(j, carry):
            body(j)
            return carry
        lax.fori_loop(first, last, step, 0)

    for k in range(SLOTS):
        pltpu.make_async_copy(tiles_ref.at[k], raw.at[k], tsem.at[k]).start()
    barrier = pltpu.get_barrier_semaphore()

    def greet(row, col):
        pl.semaphore_signal(barrier, 1, device_id=(row, col), device_id_type=MESH)

    loop(1, ROWS, lambda j: greet((r + j) % ROWS, group))

    @pl.when(owner_row != r)
    def _():
        loop(0, HALF, lambda j: greet(owner_row, owner_col + j))

    loop(1, COLS, lambda j: greet(r, (c + j) % COLS))

    def halve(k):
        wait(tsem.at[k], raw.at[k])
        tile = raw[k]
        high = tile.astype(jnp.bfloat16)
        t_high[k] = high
        t_low[k] = (tile - high.astype(jnp.float32)).astype(jnp.bfloat16)

    loop(0, SLOTS, halve)
    pl.semaphore_wait(barrier, jnp.where(owner_row != r, COLS - 1 + ROWS - 1 + HALF, COLS - 1 + ROWS - 1))

    def gather(step, src, row_exchange, col_exchange):
        dst = xc.at[step, lane_at]
        loop(1, ROWS, lambda j: send(src, dst, col_exchange, (r + j) % ROWS, group))

        @pl.when(group == c)
        def _():
            pltpu.make_async_copy(src, dst, rsem.at[col_exchange]).start()

        @pl.when(group != c)
        def _():
            send(src, dst, col_exchange, r, group)

        loop(1, COLS, lambda j: send(src, xr.at[step, c], row_exchange, r, (c + j) % COLS))
        xr[step, c] = src[...]

    def gathered(step, row_exchange, col_exchange):
        wait(rsem.at[row_exchange], xr.at[step, pl.ds(0, COLS - 1)])
        wait(rsem.at[col_exchange], xc.at[step])

    def scatter(step, fwd_exchange, bwd_exchange):
        dst = br.at[step, r]

        def one(j):
            s = (c + j) % HALF
            send(bp.at[step, s], dst, bwd_exchange, owner_row, owner_col + s)

        loop(1, HALF, one)
        mine = (owner_row == r) & (owner_col + lane_at == c)

        @pl.when(mine)
        def _():
            pltpu.make_async_copy(bp.at[step, lane_at], dst, rsem.at[bwd_exchange]).start()

        @pl.when(jnp.logical_not(mine))
        def _():
            one(0)

        def two(j):
            p = (c + j) % COLS
            send(fp.at[step, p], fr.at[step, c], fwd_exchange, r, p)

        loop(1, COLS, two)
        fr[step, c] = fp[step, c]

    def scattered(step, fwd_exchange, bwd_exchange):
        wait(rsem.at[fwd_exchange], fr.at[step, pl.ds(0, COLS - 1)])
        wait(rsem.at[bwd_exchange], br.at[step])
        return jnp.sum(fr[step], axis=0) + jnp.sum(br[step], axis=0)

    def plane_start(at, value, exchange):
        gsrc[2 * at] = value
        gp[at, c] = value
        loop(1, COLS, lambda j: send(gsrc.at[2 * at], gp.at[at, c], exchange, r, (c + j) % COLS))

    def line_start(at, plane_exchange, line_exchange):
        wait(rsem.at[plane_exchange], gp.at[at, pl.ds(0, COLS - 1)])
        value = jnp.sum(gp[at], axis=0)
        gsrc[2 * at + 1] = value
        gy[at, r] = value
        loop(1, ROWS, lambda j: send(gsrc.at[2 * at + 1], gy.at[at, r], line_exchange, (r + j) % ROWS, c))

    def line_done(at, line_exchange):
        wait(rsem.at[line_exchange], gy.at[at, pl.ds(0, ROWS - 1)])
        return jnp.sum(gy[at], axis=0)

    def products(step):
        live = count_ref[0]
        forward, backward, row_at, col_at = [], [], [], []
        cross = [jnp.zeros((8, LANES), jnp.float32) for _ in range(VEC)]
        for k in range(SLOTS):
            i, j = rows_ref[k] & (ROW_TILES - 1), cols_ref[k] & (COL_TILES - 1)
            mask = jnp.where(k < live, 1.0, 0.0).astype(jnp.float32)
            from_col, from_row = col_parts[pl.ds(2 * j, 2)], row_parts[pl.ds(2 * i, 2)]
            from_col = jnp.concatenate([from_col[0], from_col[1]], axis=1).astype(jnp.bfloat16)
            from_row = jnp.concatenate([from_row[0], from_row[1]], axis=1).astype(jnp.bfloat16)

            def multiply(block, dims):
                high = lax.dot_general(block, t_high[k], (dims, ((), ())), preferred_element_type=jnp.float32)
                low = lax.dot_general(block, t_low[k], (dims, ((), ())), preferred_element_type=jnp.float32)
                both = high + low
                left, right = both[:, :LANES], both[:, LANES:]
                left = left + pltpu.roll(left, VEC, 0)
                right = right + pltpu.roll(right, VEC, 0)
                return jnp.where(eight < VEC, left, right) * mask

            ahead = multiply(from_col, ((1,), (1,)))
            forward.append(ahead)
            backward.append(multiply(from_row, ((1,), (0,))))
            row_at.append(i)
            col_at.append(j)
            entries = row_packed[i]
            for offset in range(VEC):
                cross[offset] = cross[offset] + entries * rotated(ahead, offset)
        for values, places, out, tiles in ((backward, col_at, bp, COL_TILES), (forward, row_at, fp, ROW_TILES)):
            for t in range(tiles):
                total = jnp.where(places[0] == t, values[0], 0.0)
                for k in range(1, SLOTS):
                    total = total + jnp.where(places[k] == t, values[k], 0.0)
                out[step, 2 * t] = total[:VEC]
                out[step, 2 * t + 1] = total[VEC:]
        return cross

    gather(0, x_ref, ROW0, COL0)
    start = x_ref[...]
    start_twice = twice(start)
    half = jnp.where(eight < VEC, start_twice, 0.0)
    start_row = gram_row([half * rotated(start_twice, offset) for offset in range(VEC)])
    gathered(0, ROW0, COL0)
    for t in range(ROW_TILES):
        left, right = twice(xr[0, 2 * t]), twice(xr[0, 2 * t + 1])
        row_parts[2 * t] = split(left, eight)
        row_parts[2 * t + 1] = split(right, eight)
        row_packed[t] = jnp.where(eight < VEC, left, right)
    for s in range(HALF):
        col_parts[s] = split(twice(xc[0, s]), eight)
    cross = products(0)
    scatter(0, FWD0, BWD0)
    plane_start(0, gram_row(cross) + pltpu.roll(start_row, 16, 1), PLANE0)
    line_start(0, PLANE0, LINE0)
    image = scattered(0, FWD0, BWD0)
    own[...] = image

    gather(1, own, ROW1, COL1)
    gram = line_done(0, LINE0)
    _, inverse, inverse_t, _ = factorize(gram, 16)
    first_diag = projected(gram, inverse, inverse_t)
    first_basis = apply(inverse, start)
    from_start = -apply(first_diag, inverse)
    rest = apply(inverse, image) + apply(from_start, start)
    rest_twice = twice(rest)
    half = jnp.where(eight < VEC, rest_twice, 0.0)
    plane_start(1, gram_row([half * rotated(rest_twice, offset) for offset in range(VEC)]), PLANE1)
    inverse_twice, start_factor_twice = twice(inverse), twice(from_start)
    of_image = [jnp.broadcast_to(inverse_twice[:, j : j + 1], (8, LANES)) for j in range(VEC)]
    of_start = [jnp.broadcast_to(start_factor_twice[:, j : j + 1], (8, LANES)) for j in range(VEC)]

    def combined(ref, at):
        total = of_image[0] * ref[1, at, 0:1, :] + of_start[0] * ref[0, at, 0:1, :]
        for j in range(1, VEC):
            total = total + (of_image[j] * ref[1, at, j : j + 1, :] + of_start[j] * ref[0, at, j : j + 1, :])
        return total

    gathered(1, ROW1, COL1)
    for t in range(ROW_TILES):
        left, right = combined(xr, 2 * t), combined(xr, 2 * t + 1)
        row_parts[2 * t] = split(left, eight)
        row_parts[2 * t + 1] = split(right, eight)
        row_packed[t] = jnp.where(eight < VEC, left, right)
    for s in range(HALF):
        col_parts[s] = split(combined(xc, s), eight)
    cross = products(1)
    scatter(1, FWD1, BWD1)
    plane_start(2, gram_row(cross), PLANE2)
    line_start(1, PLANE1, LINE1)
    line_start(2, PLANE2, LINE2)
    gram = line_done(1, LINE1)
    factor, inverse, inverse_t, factor_t = factorize(gram, 0)
    next_basis = apply(inverse, rest)
    basis_ref[...] = next_basis
    image = scattered(1, FWD1, BWD1)
    known = apply(inverse, image) - apply(factor_t, first_basis)
    gram = line_done(2, LINE2)
    second_diag = projected(gram, inverse, inverse_t)
    resid_ref[...] = known - apply(second_diag, next_basis)
    coef_ref[0] = first_diag[:, :VEC]
    coef_ref[1] = second_diag[:, :VEC]
    coef_ref[2] = factor[:, :VEC]

    for step, row_exchange, col_exchange, fwd_exchange, bwd_exchange in (
        (0, ROW0, COL0, FWD0, BWD0), (1, ROW1, COL1, FWD1, BWD1)
    ):
        wait(ssem.at[row_exchange], xr.at[step, pl.ds(0, COLS - 1)])
        wait(ssem.at[fwd_exchange], fr.at[step, pl.ds(0, COLS - 1)])

        wait(ssem.at[col_exchange], xc.at[step, pl.ds(0, ROWS - 1)])

        @pl.when(group != c)
        def _():
            wait(ssem.at[col_exchange], xc.at[step, 0])

        wait(ssem.at[bwd_exchange], br.at[step, pl.ds(0, HALF - 1)])

        @pl.when(jnp.logical_not((owner_row == r) & (owner_col + lane_at == c)))
        def _():
            wait(ssem.at[bwd_exchange], br.at[step, 0])

    for at, plane_exchange, line_exchange in ((0, PLANE0, LINE0), (1, PLANE1, LINE1), (2, PLANE2, LINE2)):
        wait(ssem.at[plane_exchange], gp.at[at, pl.ds(0, COLS - 1)])
        wait(ssem.at[line_exchange], gy.at[at, pl.ds(0, ROWS - 1)])


def body(start_block, matrix_tiles, tile_rows, tile_cols, tile_counts):
    share = jax.ShapeDtypeStruct((VEC, LANES), jnp.float32)
    vmem, smem = pl.BlockSpec(memory_space=pltpu.VMEM), pl.BlockSpec(memory_space=pltpu.SMEM)
    buffer = lambda *shape: pltpu.VMEM(shape, jnp.float32)
    return pl.pallas_call(
        kernel,
        out_shape=(share, share, jax.ShapeDtypeStruct((3, VEC, VEC), jnp.float32)),
        in_specs=[vmem, pl.BlockSpec(memory_space=pl.ANY), smem, smem, smem],
        out_specs=(vmem, vmem, vmem),
        scratch_shapes=[
            buffer(SLOTS, TILE, TILE),
            pltpu.VMEM((SLOTS, TILE, TILE), jnp.bfloat16),
            pltpu.VMEM((SLOTS, TILE, TILE), jnp.bfloat16),
            buffer(VEC, LANES),
            buffer(2, COLS, VEC, LANES),
            buffer(2, HALF, VEC, LANES),
            buffer(COLS, 8, LANES),
            buffer(HALF, 8, LANES),
            buffer(ROW_TILES, 8, LANES),
            buffer(2, COLS, VEC, LANES),
            buffer(2, HALF, VEC, LANES),
            buffer(2, COLS, VEC, LANES),
            buffer(2, ROWS, VEC, LANES),
            buffer(6, 1, LANES),
            buffer(3, COLS, 1, LANES),
            buffer(3, ROWS, 1, LANES),
            pltpu.SemaphoreType.DMA((SLOTS,)),
            pltpu.SemaphoreType.DMA((14,)),
            pltpu.SemaphoreType.DMA((14,)),
        ],
        compiler_params=pltpu.CompilerParams(collective_id=0, has_side_effects=True),
    )(start_block, matrix_tiles, tile_rows, tile_cols, tile_counts)


def solution(mesh):
    return jax.shard_map(
        body,
        mesh=mesh,
        in_specs=(
            P(None, ("row", "col")),
            P(("row", "col"), None, None),
            P(("row", "col")),
            P(("row", "col")),
            P(("row", "col")),
        ),
        out_specs=(P(None, ("row", "col")), P(None, ("row", "col")), P()),
        check_vma=False,
    )
```

time: 773 us -> 65.7 us (0.08)
  waiting for transfers between devices: 378 us -> 0 us
  blocking collectives: 302 us -> 0 us
  Pallas kernels: 0 us -> 60.4 us
  matrix products: 28.5 us -> 0 us
  local copies, waits for them, and re-layouts: 25 us -> 3.76 us
  loops' own time: 18.2 us -> 0 us
  between operations: 13.9 us -> 1.29 us
    psum x2 -> x0, waiting for transfers between devices: 302 us -> none  [the longest x1 151 us: body(): lax.psum(local_products(first_basis, matrix_tiles, tile_rows, tile_cols,...]
    psum x6 -> x0, blocking collectives: 258 us -> none  [the longest x2 142 us: local_products(): column_total = lax.psum(backward, 'row')]
    all_gather x2 -> x0, waiting for transfers between devices: 76.2 us -> none  [local_products(): whole = lax.all_gather(current, 'row', axis=1, tiled=True)]
    pallas_call x0 -> x1, Pallas kernels: none -> 60.4 us  [body(): pl.pallas_call(kernel, out_shape=(share, share, jax.ShapeDtypeStruct((3,...]
    all_gather x1 -> x0, blocking collectives: 43.6 us -> none  [body(): rows_here = lax.all_gather(start_block, 'col', axis=1, tiled=True)]
    dot_general x23 -> x0, matrix products: 26.6 us -> none  [the longest x8 9.81 us: add_tile(): lax.dot_general(from_column, current_tile, (((1,), (1,)), ((), ())), prec...]
    dynamic_slice x19 -> x0, local copies, waits for them, and re-layouts: 23.4 us -> none  [the longest x8 10.6 us: add_tile(): row_start = (tile_rows[slot_index] - row_base) * tile_width]
    another operation x2 -> x0, loops' own time: 18.2 us -> none  [local_products(): forward, backward = lax.fori_loop(0, tile_counts[0], add_tile, start_state)]
  transfers between devices with their start and end apart: 4 -> 0, of which waited for: 4 -> 0; matrix products, arithmetic and copies ran while one was open for 0% -> 0% of each run, Pallas kernels for 0% -> 0%
where the time goes in v1:
time: 65.7 us; the launch traced here: 65.5 us
  Pallas kernels  60.4 us (92%)
  local copies, waits for them, and re-layouts  3.76 us (6%)
  between operations  1.29 us (2%)
    pallas_call x1, Pallas kernels, body(): pl.pallas_call(kernel, out_shape=(share, share, jax.ShapeDtypeStruct((3,...  60.4 us
    unnamed x3, local copies, waits for them, and re-layouts  3.76 us

profile of v1, /device:TPU:1, one launch (start us, length us, event | category | flops | bytes accessed | tf_op | source)
XLA Modules:
  0.0 65.5 jit_solution(7047854842523878476)
XLA Ops:
  1.3 60.4 %shard_map.76 = (f32[4,128]{1,0:T(4,128)}, f32[4,128]{1,0:T(4,128)}, f32[3,4,4]{2,1,0:T(4,128)}) custom-call(f32[4,128]{1,0:T(4,128)} %x_ref.1, f32[8,256,256]{2,1,0:T(8,128)} %tiles_ref.1, s32[8]{0:T(128)} %rows_ref.1, s32[8]{0:T(128)} %cols_ref.1, s32[1]{0:T(128)S(6)} %copy.11.count_ref), custom_call_target="tpu_custom_call" | custom-call | tf_op jit(solution)/shard_map/pallas_call | solution.py:346
  61.7 1.2 %copy.12 = f32[4,128]{1,0:T(4,128)} copy(f32[4,128]{1,0:T(4,128)} %get-tuple-element.6) | data formatting | bytes 4096
  62.9 1.2 %copy.13 = f32[4,128]{1,0:T(4,128)} copy(f32[4,128]{1,0:T(4,128)} %get-tuple-element.7) | data formatting | bytes 4096
  64.2 1.3 %copy.14 = f32[3,4,4]{2,1,0:T(4,128)} copy(f32[3,4,4]{2,1,0:T(4,128)} %get-tuple-element.8) | data formatting | bytes 384

commit v2 on v1

v2 whole, which is shorter than its diff:
```python
import jax
import jax.numpy as jnp
from jax import lax
from jax.experimental import pallas as pl
from jax.experimental.pallas import tpu as pltpu
from jax.sharding import PartitionSpec as P

MESH = pl.DeviceIdType.MESH
epsilon = 1e-06
VEC, TILE, SLOTS, LANES = 4, 256, 8, 128
ROWS, COLS = 16, 32
HALF = COLS // 2
ROW_TILES, COL_TILES = 16, 8
ORDER = ROWS * COLS * LANES

ROW0, COL0, FWD0, BWD0, ROW1, COL1, FWD1, BWD1, PLANE0, LINE0, PLANE1, LINE1, PLANE2, LINE2 = range(14)


def iota(shape, axis):
    return lax.broadcasted_iota(jnp.int32, shape, axis)


def apply(matrix, block):
    return sum(matrix[:, j : j + 1] * block[j : j + 1, :] for j in range(VEC))


def rotated(block, offset):
    if offset == 0:
        return block
    keep = iota((8, LANES), 0) % VEC + offset < VEC
    return jnp.where(keep, pltpu.roll(block, 8 - offset, 0), pltpu.roll(block, VEC - offset, 0))


def gram_row(products):
    total = jnp.zeros((8, LANES), jnp.float32)
    lane, row = iota((8, LANES), 1), iota((8, LANES), 0)
    for offset, product in enumerate(products):
        summed = jnp.sum(product, axis=1, keepdims=True)
        total = jnp.where(lane == VEC * offset + row % VEC, summed, total)
    return jnp.sum(total, axis=0, keepdims=True)


def entry(gram, base, i, j):
    lane = base + VEC * ((j - i) % VEC) + i
    return gram[:, lane : lane + 1]


def assemble(entries):
    lane, row = iota((VEC, LANES), 1), iota((VEC, LANES), 0)
    total = jnp.zeros((VEC, LANES), jnp.float32)
    for (i, j), value in entries.items():
        total = jnp.where((row == i) & (lane == j), value, total)
    return total


def factorize(gram, base):
    a = {(i, j): entry(gram, base, i, j) * (1.0 / ORDER) for i in range(VEC) for j in range(i + 1)}
    low, inv = {}, {}
    for j in range(VEC):
        pivot = a[j, j] + epsilon
        for k in range(j):
            pivot = pivot - low[j, k] * low[j, k]
        low[j, j] = jnp.sqrt(pivot)
        inv[j, j] = 1.0 / low[j, j]
        for i in range(j + 1, VEC):
            rest = a[i, j]
            for k in range(j):
                rest = rest - low[i, k] * low[j, k]
            low[i, j] = rest * inv[j, j]
    for j in range(VEC):
        for i in range(j + 1, VEC):
            rest = low[i, j] * inv[j, j]
            for k in range(j + 1, i):
                rest = rest + low[i, k] * inv[k, j]
            inv[i, j] = -rest * inv[i, i]
    flip = lambda entries: {(j, i): value for (i, j), value in entries.items()}
    return assemble(low), assemble(inv), assemble(flip(inv)), assemble(flip(low))


def projected(gram, inverse, inverse_t):
    entries = {}
    for i in range(VEC):
        for j in range(i + 1):
            value = (entry(gram, 0, i, j) + entry(gram, 0, j, i)) * (1.0 / ORDER)
            entries[i, j] = value
            entries[j, i] = value
    return apply(apply(inverse, assemble(entries)), inverse_t)


def split(block, row):
    high = block.astype(jnp.bfloat16).astype(jnp.float32)
    return jnp.where(row < VEC, high, block - high)


def twice(block):
    return jnp.concatenate([block, block], axis=0)


def kernel(
    x_hbm, tiles_hbm, rows_hbm, cols_hbm, count_hbm,
    basis_ref, resid_ref, coef_ref,
    x_ref, rows_ref, cols_ref, count_ref, raw, t_high, t_low, own, xr, xc, row_parts, col_parts, row_packed,
    fp, bp, fr, br, fm, bm, gsrc, gy, gp, isem, tsem, ssem, rsem,
):
    r, c = lax.axis_index("row"), lax.axis_index("col")
    y, core, z, x = lax.div(r, 2), lax.rem(r, 2), lax.div(c, 4), lax.rem(c, 4)
    group = 2 * r + lax.div(c, HALF)
    owner_row, owner_col = lax.div(c, 2), HALF * lax.rem(c, 2)
    lane_at = lax.rem(c, HALF)
    eight = iota((8, LANES), 0)

    turn = lax.rem(x + 4 - 2 * core, 4)
    odd = jnp.where((turn == 1) | (turn == 2), 1, 0)
    near = lax.rem(z + 9 - y, 8)
    keeper = near < 4
    kept_pair = jnp.where(keeper, near, 0) + jnp.where(turn >= 2, 4, 0)
    kept_group = 2 * r + odd

    def keeper_col(g, q):
        at_z = lax.rem(lax.div(g, 4) + 7 + lax.rem(q, 4), 8)
        at_x = lax.rem(g + 4 + (2 * lax.rem(g, 2) - 1) * lax.div(q, 4), 4)
        return 4 * at_z + at_x

    def send(src, dst, exchange, row, col):
        pltpu.make_async_remote_copy(
            src_ref=src, dst_ref=dst, send_sem=ssem.at[exchange], recv_sem=rsem.at[exchange],
            device_id=(row, col), device_id_type=MESH,
        ).start()

    def send_or_keep(src, dst, exchange, row, col):
        mine = (row == r) & (col == c)

        @pl.when(mine)
        def _():
            pltpu.make_async_copy(src, dst, rsem.at[exchange]).start()

        @pl.when(jnp.logical_not(mine))
        def _():
            send(src, dst, exchange, row, col)

    def wait(sem, ref):
        pltpu.make_async_copy(ref, ref, sem).wait()

    def loop(first, last, body):
        def step(j, carry):
            body(j)
            return carry
        lax.fori_loop(first, last, step, 0)

    pending = []

    pltpu.make_async_copy(x_hbm, x_ref, isem.at[0]).start()
    barrier = pltpu.get_barrier_semaphore()

    def greet(row, col):
        pl.semaphore_signal(barrier, 1, device_id=(row, col), device_id_type=MESH)

    loop(1, ROWS, lambda j: greet(lax.rem(r + j, ROWS), group))

    @pl.when(owner_row != r)
    def _():
        loop(0, HALF, lambda j: greet(owner_row, owner_col + j))

    loop(1, COLS, lambda j: greet(r, lax.rem(c + j, COLS)))
    for k in range(SLOTS):
        pltpu.make_async_copy(tiles_hbm.at[k], raw.at[k], tsem.at[k]).start()
    pltpu.make_async_copy(rows_hbm, rows_ref, isem.at[1]).start()
    pltpu.make_async_copy(cols_hbm, cols_ref, isem.at[2]).start()
    pltpu.make_async_copy(count_hbm, count_ref, isem.at[3]).start()
    wait(isem.at[0], x_ref)
    pl.semaphore_wait(barrier, jnp.where(owner_row != r, COLS - 1 + ROWS - 1 + HALF, COLS - 1 + ROWS - 1))

    def line_start(at, value, exchange):
        gsrc[2 * at] = value
        gy[at, r] = value
        loop(1, ROWS, lambda j: send(gsrc.at[2 * at], gy.at[at, r], exchange, lax.rem(r + j, ROWS), c))
        pending.append((exchange, gy.at[at, pl.ds(0, ROWS - 1)], None))

    def plane_start(at, line_exchange, exchange):
        wait(rsem.at[line_exchange], gy.at[at, pl.ds(0, ROWS - 1)])
        value = jnp.sum(gy[at], axis=0)
        gsrc[2 * at + 1] = value
        gp[at, c] = value
        loop(1, COLS, lambda j: send(gsrc.at[2 * at + 1], gp.at[at, c], exchange, r, lax.rem(c + j, COLS)))
        pending.append((exchange, gp.at[at, pl.ds(0, COLS - 1)], None))

    def plane_done(at, exchange):
        wait(rsem.at[exchange], gp.at[at, pl.ds(0, COLS - 1)])
        return jnp.sum(gp[at], axis=0)

    def spread(step, values, places, out, tiles):
        for t in range(tiles):
            total = jnp.where(places[0] == t, values[0], 0.0)
            for k in range(1, SLOTS):
                total = total + jnp.where(places[k] == t, values[k], 0.0)
            out[step, 2 * t] = total[:VEC]
            out[step, 2 * t + 1] = total[VEC:]

    def places():
        row_at = [lax.rem(rows_ref[k], ROW_TILES) for k in range(SLOTS)]
        col_at = [lax.rem(cols_ref[k], COL_TILES) for k in range(SLOTS)]
        masks = [jnp.where(k < count_ref[0], 1.0, 0.0).astype(jnp.float32) for k in range(SLOTS)]
        return row_at, col_at, masks

    def multiply(k, parts, at, dims, mask):
        block = parts[pl.ds(2 * at, 2)]
        block = jnp.concatenate([block[0], block[1]], axis=1).astype(jnp.bfloat16)
        high = lax.dot_general(block, t_high[k], (dims, ((), ())), preferred_element_type=jnp.float32)
        low = lax.dot_general(block, t_low[k], (dims, ((), ())), preferred_element_type=jnp.float32)
        both = high + low
        left, right = both[:, :LANES], both[:, LANES:]
        left = left + pltpu.roll(left, VEC, 0)
        right = right + pltpu.roll(right, VEC, 0)
        return jnp.where(eight < VEC, left, right) * mask

    def crossed(forward, row_at):
        cross = [jnp.zeros((8, LANES), jnp.float32) for _ in range(VEC)]
        for k in range(SLOTS):
            entries = row_packed[row_at[k]]
            for offset in range(VEC):
                cross[offset] = cross[offset] + entries * rotated(forward[k], offset)
        return gram_row(cross)

    def own_gram(block):
        block = twice(block)
        half = jnp.where(eight < VEC, block, 0.0)
        return gram_row([half * rotated(block, offset) for offset in range(VEC)])

    dst = xc.at[0, lane_at]
    loop(1, ROWS, lambda j: send(x_ref, dst, COL0, lax.rem(r + j, ROWS), group))
    send_or_keep(x_ref, dst, COL0, r, group)
    loop(1, COLS, lambda j: send(x_ref, xr.at[0, c], ROW0, r, lax.rem(c + j, COLS)))
    start = x_ref[...]
    xr[0, c] = start
    pending.append((ROW0, xr.at[0, pl.ds(0, COLS - 1)], None))
    pending.append((COL0, xc.at[0, pl.ds(0, ROWS - 1)], None))
    pending.append((COL0, xc.at[0, 0], group != c))

    def halve(k):
        wait(tsem.at[k], raw.at[k])
        tile = raw[k]
        high = tile.astype(jnp.bfloat16)
        t_high[k] = high
        t_low[k] = (tile - high.astype(jnp.float32)).astype(jnp.bfloat16)

    loop(0, SLOTS, halve)
    wait(isem.at[1], rows_ref)
    wait(isem.at[2], cols_ref)
    wait(isem.at[3], count_ref)
    row_at, col_at, masks = places()
    start_row = pltpu.roll(own_gram(start), 16, 1)
    wait(rsem.at[ROW0], xr.at[0, pl.ds(0, COLS - 1)])
    for t in range(ROW_TILES):
        left, right = twice(xr[0, 2 * t]), twice(xr[0, 2 * t + 1])
        row_parts[2 * t] = split(left, eight)
        row_parts[2 * t + 1] = split(right, eight)
        row_packed[t] = jnp.where(eight < VEC, left, right)
    wait(rsem.at[COL0], xc.at[0])
    for s in range(HALF):
        col_parts[s] = split(twice(xc[0, s]), eight)
    backward = [multiply(k, row_parts, row_at[k], ((1,), (0,)), masks[k]) for k in range(SLOTS)]
    spread(0, backward, col_at, bp, COL_TILES)

    loop(0, 8, lambda q: send_or_keep(bp.at[0, pl.ds(2 * q, 2)], bm.at[r], BWD0, owner_row, keeper_col(c, q)))
    forward = [multiply(k, col_parts, col_at[k], ((1,), (1,)), masks[k]) for k in range(SLOTS)]
    spread(0, forward, row_at, fp, ROW_TILES)
    loop(0, HALF, lambda q: send_or_keep(
        fp.at[0, pl.ds(2 * q, 2)], fm.at[c], FWD0, r, keeper_col(2 * r + lax.div(q, 8), lax.rem(q, 8))))
    pending.append((BWD0, bp.at[0, pl.ds(0, HALF - 2)], None))
    pending.append((BWD0, bp.at[0, pl.ds(0, 2)], jnp.logical_not(keeper & (kept_group == c))))
    pending.append((FWD0, fp.at[0, pl.ds(0, COLS - 2)], None))
    pending.append((FWD0, fp.at[0, pl.ds(0, 2)], jnp.logical_not(keeper)))
    line_start(0, crossed(forward, row_at) + start_row, LINE0)

    at_row = xr.at[1, pl.ds(HALF * odd + 2 * kept_pair, 2)]
    at_col = xc.at[1, pl.ds(2 * kept_pair, 2)]

    @pl.when(keeper)
    def _():
        wait(rsem.at[FWD0], fm)
        ahead = jnp.sum(fm[...], axis=0)
        wait(rsem.at[BWD0], bm)
        own[...] = ahead + jnp.sum(bm[...], axis=0)
        loop(0, ROWS, lambda j: send_or_keep(own, at_col, COL1, lax.rem(r + j, ROWS), kept_group))
        loop(1, COLS, lambda j: send(own, at_row, ROW1, r, lax.rem(c + j, COLS)))
        pltpu.make_async_copy(own, at_row, rsem.at[ROW1]).start()

    for lap in range(2):
        pending.append((ROW1, xr.at[1, pl.ds(0, COLS - 1)], keeper))
    pending.append((COL1, xc.at[1, pl.ds(0, HALF)], keeper))
    pending.append((COL1, xc.at[1, pl.ds(0, HALF - 2)], keeper))
    pending.append((COL1, xc.at[1, pl.ds(0, 2)], keeper & (kept_group != c)))

    plane_start(0, LINE0, PLANE0)
    gram = plane_done(0, PLANE0)
    _, inverse, inverse_t, _ = factorize(gram, 16)
    first_diag = projected(gram, inverse, inverse_t)
    first_basis = apply(inverse, start)
    from_start = -apply(first_diag, inverse)
    inverse_twice, start_factor_twice = twice(inverse), twice(from_start)
    of_image = [jnp.broadcast_to(inverse_twice[:, j : j + 1], (8, LANES)) for j in range(VEC)]
    of_start = [jnp.broadcast_to(start_factor_twice[:, j : j + 1], (8, LANES)) for j in range(VEC)]

    def combined(ref, at):
        total = of_image[0] * ref[1, at, 0:1, :] + of_start[0] * ref[0, at, 0:1, :]
        for j in range(1, VEC):
            total = total + (of_image[j] * ref[1, at, j : j + 1, :] + of_start[j] * ref[0, at, j : j + 1, :])
        return total

    wait(rsem.at[ROW1], xr.at[1])
    rest = apply(inverse, xr[1, c]) + apply(from_start, start)
    rest_row = own_gram(rest)
    line_start(1, rest_row, LINE1)
    for t in range(ROW_TILES):
        left, right = combined(xr, 2 * t), combined(xr, 2 * t + 1)
        row_parts[2 * t] = split(left, eight)
        row_parts[2 * t + 1] = split(right, eight)
        row_packed[t] = jnp.where(eight < VEC, left, right)
    wait(rsem.at[COL1], xc.at[1])
    for s in range(HALF):
        col_parts[s] = split(combined(xc, s), eight)
    forward = [multiply(k, col_parts, col_at[k], ((1,), (1,)), masks[k]) for k in range(SLOTS)]
    line_start(2, crossed(forward, row_at), LINE2)
    backward = [multiply(k, row_parts, row_at[k], ((1,), (0,)), masks[k]) for k in range(SLOTS)]
    spread(1, backward, col_at, bp, COL_TILES)

    def back(j):
        s = lax.rem(c + j, HALF)
        send_or_keep(bp.at[1, s], br.at[r], BWD1, owner_row, owner_col + s)

    loop(0, HALF, back)
    spread(1, forward, row_at, fp, ROW_TILES)

    def ahead(j):
        p = lax.rem(c + j, COLS)
        send(fp.at[1, p], fr.at[c], FWD1, r, p)

    loop(1, COLS, ahead)
    fr[c] = fp[1, c]
    pending.append((FWD1, fr.at[pl.ds(0, COLS - 1)], None))
    pending.append((BWD1, br.at[pl.ds(0, HALF - 1)], None))
    pending.append((BWD1, br.at[0], group != c))
    plane_start(1, LINE1, PLANE1)
    plane_start(2, LINE2, PLANE2)
    gram = plane_done(1, PLANE1)
    factor, inverse, inverse_t, factor_t = factorize(gram, 0)
    next_basis = apply(inverse, rest)
    basis_ref[...] = next_basis
    wait(rsem.at[FWD1], fr.at[pl.ds(0, COLS - 1)])
    image = jnp.sum(fr[...], axis=0)
    wait(rsem.at[BWD1], br)
    image = image + jnp.sum(br[...], axis=0)
    known = apply(inverse, image) - apply(factor_t, first_basis)
    for exchange, ref, condition in pending[:-1]:
        if condition is None:
            wait(ssem.at[exchange], ref)
        else:
            pl.when(condition)(lambda exchange=exchange, ref=ref: wait(ssem.at[exchange], ref))
    gram = plane_done(2, PLANE2)
    second_diag = projected(gram, inverse, inverse_t)
    resid_ref[...] = known - apply(second_diag, next_basis)
    coef_ref[0] = first_diag[:, :VEC]
    coef_ref[1] = second_diag[:, :VEC]
    coef_ref[2] = factor[:, :VEC]
    wait(ssem.at[pending[-1][0]], pending[-1][1])


def settle(basis, resid, coef, basis_out, resid_out, coef_out, sem):
    copies = [
        pltpu.make_async_copy(src, dst, sem.at[at])
        for at, (src, dst) in enumerate(((basis, basis_out), (resid, resid_out), (coef, coef_out)))
    ]
    for copy in copies:
        copy.start()
    for copy in copies:
        copy.wait()


def body(start_block, matrix_tiles, tile_rows, tile_cols, tile_counts):
    share = jax.ShapeDtypeStruct((VEC, LANES), jnp.float32)
    shapes = (share, share, jax.ShapeDtypeStruct((3, VEC, VEC), jnp.float32))
    vmem, anywhere = pl.BlockSpec(memory_space=pltpu.VMEM), pl.BlockSpec(memory_space=pl.ANY)
    buffer = lambda *shape: pltpu.VMEM(shape, jnp.float32)
    found = pl.pallas_call(
        kernel,
        out_shape=shapes,
        in_specs=[anywhere] * 5,
        out_specs=(vmem, vmem, vmem),
        scratch_shapes=[
            buffer(VEC, LANES),
            pltpu.SMEM((SLOTS,), jnp.int32),
            pltpu.SMEM((SLOTS,), jnp.int32),
            pltpu.SMEM((1,), jnp.int32),
            buffer(SLOTS, TILE, TILE),
            pltpu.VMEM((SLOTS, TILE, TILE), jnp.bfloat16),
            pltpu.VMEM((SLOTS, TILE, TILE), jnp.bfloat16),
            buffer(2, VEC, LANES),
            buffer(2, COLS, VEC, LANES),
            buffer(2, HALF, VEC, LANES),
            buffer(COLS, 8, LANES),
            buffer(HALF, 8, LANES),
            buffer(ROW_TILES, 8, LANES),
            buffer(2, COLS, VEC, LANES),
            buffer(2, HALF, VEC, LANES),
            buffer(COLS, VEC, LANES),
            buffer(ROWS, VEC, LANES),
            buffer(COLS, 2, VEC, LANES),
            buffer(ROWS, 2, VEC, LANES),
            buffer(6, 1, LANES),
            buffer(3, ROWS, 1, LANES),
            buffer(3, COLS, 1, LANES),
            pltpu.SemaphoreType.DMA((4,)),
            pltpu.SemaphoreType.DMA((SLOTS,)),
            pltpu.SemaphoreType.DMA((14,)),
            pltpu.SemaphoreType.DMA((14,)),
        ],
        compiler_params=pltpu.CompilerParams(collective_id=0, has_side_effects=True),
    )(start_block, matrix_tiles, tile_rows, tile_cols, tile_counts)
    return pl.pallas_call(
        settle,
        out_shape=shapes,
        in_specs=[anywhere] * 3,
        out_specs=(anywhere, anywhere, anywhere),
        scratch_shapes=[pltpu.SemaphoreType.DMA((3,))],
    )(*found)


def solution(mesh):
    return jax.shard_map(
        body,
        mesh=mesh,
        in_specs=(
            P(None, ("row", "col")),
            P(("row", "col"), None, None),
            P(("row", "col")),
            P(("row", "col")),
            P(("row", "col")),
        ),
        out_specs=(P(None, ("row", "col")), P(None, ("row", "col")), P()),
        check_vma=False,
    )
```

time: 65.7 us -> 57.8 us (0.88)
  Pallas kernels: 60.4 us -> 56.4 us
  local copies, waits for them, and re-layouts: 3.76 us -> 0 us
    pallas_call x1 -> x2, Pallas kernels: 60.4 us -> 56.4 us  [the longest x1 54.9 us: body(): pl.pallas_call(kernel, out_shape=shapes, in_specs=[anywhere] * 5, out_spe...]
    unnamed x3 -> x0, local copies, waits for them, and re-layouts: 3.76 us -> none
where the time goes in v2:
time: 57.8 us; the launch traced here: 57.6 us
  Pallas kernels  56.4 us (98%)
  between operations  1.29 us (2%)
    pallas_call x1, Pallas kernels, body(): pl.pallas_call(kernel, out_shape=shapes, in_specs=[anywhere] * 5, out_spe...  54.9 us
    pallas_call x1, Pallas kernels, body(): pl.pallas_call(settle, out_shape=shapes, in_specs=[anywhere] * 3, out_spe...  1.44 us

profile of v2, /device:TPU:1, one launch (start us, length us, event | category | flops | bytes accessed | tf_op | source)
XLA Modules:
  0.0 57.6 jit_solution(9846137870370350462)
XLA Ops:
  1.3 54.9 %shard_map.76 = (f32[4,128]{1,0:T(4,128)}, f32[4,128]{1,0:T(4,128)}, f32[3,4,4]{2,1,0:T(4,128)}) custom-call(f32[4,128]{1,0:T(4,128)} %x_hbm.1, f32[8,256,256]{2,1,0:T(8,128)} %tiles_hbm.1, s32[8]{0:T(128)} %rows_hbm.1, s32[8]{0:T(128)} %cols_hbm.1, s32[1]{0:T(128)S(6)} %copy.8.count_hbm), custom_call_target="tpu_custom_call" | custom-call | tf_op jit(solution)/shard_map/pallas_call | solution.py:384
  56.2 1.4 %shard_map.77 = (f32[4,128]{1,0:T(4,128)}, f32[4,128]{1,0:T(4,128)}, f32[3,4,4]{2,1,0:T(4,128)}) custom-call(f32[4,128]{1,0:T(4,128)} %get-tuple-element.6.basis, f32[4,128]{1,0:T(4,128)} %get-tuple-element.7.resid, f32[3,4,4]{2,1,0:T(4,128)} %get-tuple-element.8.coef), custom_call_target="tpu_custom_call" | custom-call | tf_op jit(solution)/shard_map/pallas_call | solution.py:419

commit v3 on v2

--- a/solution.py
+++ b/solution.py
@@ -99,7 +99,7 @@
 def kernel(
     x_hbm, tiles_hbm, rows_hbm, cols_hbm, count_hbm,
     basis_ref, resid_ref, coef_ref,
-    x_ref, rows_ref, cols_ref, count_ref, raw, t_high, t_low, own, xr, xc, row_parts, col_parts, row_packed,
+    x_ref, rows_ref, cols_ref, count_ref, raw, t_high, t_low, own, xr, xc, row_parts, col_parts, col_packed,
     fp, bp, fr, br, fm, bm, gsrc, gy, gp, isem, tsem, ssem, rsem,
 ):
     r, c = lax.axis_index("row"), lax.axis_index("col")
@@ -147,6 +147,19 @@
             return carry
         lax.fori_loop(first, last, step, 0)
 
+    def outward(j, size):
+        return size // 2 + lax.div(j + 1, 2) * (1 - 2 * lax.rem(j, 2))
+
+    def over_plane(body):
+        def one(j):
+            body(4 * lax.rem(z + outward(lax.div(j, 4), 8), 8) + lax.rem(x + outward(lax.rem(j, 4), 4), 4))
+        loop(0, COLS - 1, one)
+
+    def over_line(body, count=ROWS - 1):
+        def one(j):
+            body(2 * lax.rem(y + outward(lax.div(j, 2), 8), 8) + lax.rem(core + 1 + lax.rem(j, 2), 2))
+        loop(0, count, one)
+
     pending = []
 
     pltpu.make_async_copy(x_hbm, x_ref, isem.at[0]).start()
@@ -155,13 +168,13 @@
     def greet(row, col):
         pl.semaphore_signal(barrier, 1, device_id=(row, col), device_id_type=MESH)
 
-    loop(1, ROWS, lambda j: greet(lax.rem(r + j, ROWS), group))
+    over_line(lambda row: greet(row, group))
 
     @pl.when(owner_row != r)
     def _():
         loop(0, HALF, lambda j: greet(owner_row, owner_col + j))
 
-    loop(1, COLS, lambda j: greet(r, lax.rem(c + j, COLS)))
+    over_plane(lambda col: greet(r, col))
     for k in range(SLOTS):
         pltpu.make_async_copy(tiles_hbm.at[k], raw.at[k], tsem.at[k]).start()
     pltpu.make_async_copy(rows_hbm, rows_ref, isem.at[1]).start()
@@ -173,7 +186,7 @@
     def line_start(at, value, exchange):
         gsrc[2 * at] = value
         gy[at, r] = value
-        loop(1, ROWS, lambda j: send(gsrc.at[2 * at], gy.at[at, r], exchange, lax.rem(r + j, ROWS), c))
+        over_line(lambda row: send(gsrc.at[2 * at], gy.at[at, r], exchange, row, c))
         pending.append((exchange, gy.at[at, pl.ds(0, ROWS - 1)], None))
 
     def plane_start(at, line_exchange, exchange):
@@ -181,7 +194,7 @@
         value = jnp.sum(gy[at], axis=0)
         gsrc[2 * at + 1] = value
         gp[at, c] = value
-        loop(1, COLS, lambda j: send(gsrc.at[2 * at + 1], gp.at[at, c], exchange, r, lax.rem(c + j, COLS)))
+        over_plane(lambda col: send(gsrc.at[2 * at + 1], gp.at[at, c], exchange, r, col))
         pending.append((exchange, gp.at[at, pl.ds(0, COLS - 1)], None))
 
     def plane_done(at, exchange):
@@ -213,12 +226,12 @@
         right = right + pltpu.roll(right, VEC, 0)
         return jnp.where(eight < VEC, left, right) * mask
 
-    def crossed(forward, row_at):
+    def crossed(backward, col_at):
         cross = [jnp.zeros((8, LANES), jnp.float32) for _ in range(VEC)]
         for k in range(SLOTS):
-            entries = row_packed[row_at[k]]
+            entries = col_packed[col_at[k]]
             for offset in range(VEC):
-                cross[offset] = cross[offset] + entries * rotated(forward[k], offset)
+                cross[offset] = cross[offset] + entries * rotated(backward[k], offset)
         return gram_row(cross)
 
     def own_gram(block):
@@ -227,9 +240,9 @@
         return gram_row([half * rotated(block, offset) for offset in range(VEC)])
 
     dst = xc.at[0, lane_at]
-    loop(1, ROWS, lambda j: send(x_ref, dst, COL0, lax.rem(r + j, ROWS), group))
+    over_line(lambda row: send(x_ref, dst, COL0, row, group))
     send_or_keep(x_ref, dst, COL0, r, group)
-    loop(1, COLS, lambda j: send(x_ref, xr.at[0, c], ROW0, r, lax.rem(c + j, COLS)))
+    over_plane(lambda col: send(x_ref, xr.at[0, c], ROW0, r, col))
     start = x_ref[...]
     xr[0, c] = start
     pending.append((ROW0, xr.at[0, pl.ds(0, COLS - 1)], None))
@@ -250,18 +263,22 @@
     row_at, col_at, masks = places()
     start_row = pltpu.roll(own_gram(start), 16, 1)
     wait(rsem.at[ROW0], xr.at[0, pl.ds(0, COLS - 1)])
-    for t in range(ROW_TILES):
-        left, right = twice(xr[0, 2 * t]), twice(xr[0, 2 * t + 1])
-        row_parts[2 * t] = split(left, eight)
-        row_parts[2 * t + 1] = split(right, eight)
-        row_packed[t] = jnp.where(eight < VEC, left, right)
-    wait(rsem.at[COL0], xc.at[0])
-    for s in range(HALF):
-        col_parts[s] = split(twice(xc[0, s]), eight)
+    for t in range(COLS):
+        row_parts[t] = split(twice(xr[0, t]), eight)
     backward = [multiply(k, row_parts, row_at[k], ((1,), (0,)), masks[k]) for k in range(SLOTS)]
     spread(0, backward, col_at, bp, COL_TILES)
 
-    loop(0, 8, lambda q: send_or_keep(bp.at[0, pl.ds(2 * q, 2)], bm.at[r], BWD0, owner_row, keeper_col(c, q)))
+    def to_keeper(j):
+        send_or_keep(bp.at[0, pl.ds(14 - 2 * j, 2)], bm.at[r], BWD0, owner_row, keeper_col(c, 7 - j))
+
+    loop(0, 8, to_keeper)
+    wait(rsem.at[COL0], xc.at[0])
+    for t in range(COL_TILES):
+        left, right = twice(xc[0, 2 * t]), twice(xc[0, 2 * t + 1])
+        col_parts[2 * t] = split(left, eight)
+        col_parts[2 * t + 1] = split(right, eight)
+        col_packed[t] = jnp.where(eight < VEC, left, right)
+    line_start(0, crossed(backward, col_at) + start_row, LINE0)
     forward = [multiply(k, col_parts, col_at[k], ((1,), (1,)), masks[k]) for k in range(SLOTS)]
     spread(0, forward, row_at, fp, ROW_TILES)
     loop(0, HALF, lambda q: send_or_keep(
@@ -270,19 +287,20 @@
     pending.append((BWD0, bp.at[0, pl.ds(0, 2)], jnp.logical_not(keeper & (kept_group == c))))
     pending.append((FWD0, fp.at[0, pl.ds(0, COLS - 2)], None))
     pending.append((FWD0, fp.at[0, pl.ds(0, 2)], jnp.logical_not(keeper)))
-    line_start(0, crossed(forward, row_at) + start_row, LINE0)
-
-    at_row = xr.at[1, pl.ds(HALF * odd + 2 * kept_pair, 2)]
+    plane_start(0, LINE0, PLANE0)
+
+    kept_at = HALF * odd + 2 * kept_pair
+    at_row = xr.at[1, pl.ds(kept_at, 2)]
     at_col = xc.at[1, pl.ds(2 * kept_pair, 2)]
 
     @pl.when(keeper)
     def _():
         wait(rsem.at[FWD0], fm)
-        ahead = jnp.sum(fm[...], axis=0)
+        total = jnp.sum(fm[...], axis=0)
         wait(rsem.at[BWD0], bm)
-        own[...] = ahead + jnp.sum(bm[...], axis=0)
-        loop(0, ROWS, lambda j: send_or_keep(own, at_col, COL1, lax.rem(r + j, ROWS), kept_group))
-        loop(1, COLS, lambda j: send(own, at_row, ROW1, r, lax.rem(c + j, COLS)))
+        own[...] = total + jnp.sum(bm[...], axis=0)
+        over_line(lambda row: send_or_keep(own, at_col, COL1, row, kept_group), ROWS)
+        over_plane(lambda col: send(own, at_row, ROW1, r, col))
         pltpu.make_async_copy(own, at_row, rsem.at[ROW1]).start()
 
     for lap in range(2):
@@ -291,7 +309,6 @@
     pending.append((COL1, xc.at[1, pl.ds(0, HALF - 2)], keeper))
     pending.append((COL1, xc.at[1, pl.ds(0, 2)], keeper & (kept_group != c)))
 
-    plane_start(0, LINE0, PLANE0)
     gram = plane_done(0, PLANE0)
     _, inverse, inverse_t, _ = factorize(gram, 16)
     first_diag = projected(gram, inverse, inverse_t)
@@ -307,20 +324,12 @@
             total = total + (of_image[j] * ref[1, at, j : j + 1, :] + of_start[j] * ref[0, at, j : j + 1, :])
         return total
 
+    kept = [apply(inverse, own[at]) + apply(from_start, xr[0, kept_at + at]) for at in range(2)]
+    rest_row = own_gram(kept[0]) + own_gram(kept[1])
+    line_start(1, jnp.where(keeper, rest_row, 0.0), LINE1)
     wait(rsem.at[ROW1], xr.at[1])
-    rest = apply(inverse, xr[1, c]) + apply(from_start, start)
-    rest_row = own_gram(rest)
-    line_start(1, rest_row, LINE1)
-    for t in range(ROW_TILES):
-        left, right = combined(xr, 2 * t), combined(xr, 2 * t + 1)
-        row_parts[2 * t] = split(left, eight)
-        row_parts[2 * t + 1] = split(right, eight)
-        row_packed[t] = jnp.where(eight < VEC, left, right)
-    wait(rsem.at[COL1], xc.at[1])
-    for s in range(HALF):
-        col_parts[s] = split(combined(xc, s), eight)
-    forward = [multiply(k, col_parts, col_at[k], ((1,), (1,)), masks[k]) for k in range(SLOTS)]
-    line_start(2, crossed(forward, row_at), LINE2)
+    for t in range(COLS):
+        row_parts[t] = split(combined(xr, t), eight)
     backward = [multiply(k, row_parts, row_at[k], ((1,), (0,)), masks[k]) for k in range(SLOTS)]
     spread(1, backward, col_at, bp, COL_TILES)
 
@@ -329,13 +338,16 @@
         send_or_keep(bp.at[1, s], br.at[r], BWD1, owner_row, owner_col + s)
 
     loop(0, HALF, back)
+    wait(rsem.at[COL1], xc.at[1])
+    for t in range(COL_TILES):
+        left, right = combined(xc, 2 * t), combined(xc, 2 * t + 1)
+        col_parts[2 * t] = split(left, eight)
+        col_parts[2 * t + 1] = split(right, eight)
+        col_packed[t] = jnp.where(eight < VEC, left, right)
+    line_start(2, crossed(backward, col_at), LINE2)
+    forward = [multiply(k, col_parts, col_at[k], ((1,), (1,)), masks[k]) for k in range(SLOTS)]
     spread(1, forward, row_at, fp, ROW_TILES)
-
-    def ahead(j):
-        p = lax.rem(c + j, COLS)
-        send(fp.at[1, p], fr.at[c], FWD1, r, p)
-
-    loop(1, COLS, ahead)
+    over_plane(lambda col: send(fp.at[1, col], fr.at[c], FWD1, r, col))
     fr[c] = fp[1, c]
     pending.append((FWD1, fr.at[pl.ds(0, COLS - 1)], None))
     pending.append((BWD1, br.at[pl.ds(0, HALF - 1)], None))
@@ -343,6 +355,7 @@
     plane_start(1, LINE1, PLANE1)
     plane_start(2, LINE2, PLANE2)
     gram = plane_done(1, PLANE1)
+    rest = apply(inverse, xr[1, c]) + apply(from_start, start)
     factor, inverse, inverse_t, factor_t = factorize(gram, 0)
     next_basis = apply(inverse, rest)
     basis_ref[...] = next_basis
@@ -383,7 +396,7 @@
     buffer = lambda *shape: pltpu.VMEM(shape, jnp.float32)
     found = pl.pallas_call(
         kernel,
-        out_shape=shapes,
+        out_shape=tuple(pltpu.VMEM(shape.shape, shape.dtype) for shape in shapes),
         in_specs=[anywhere] * 5,
         out_specs=(vmem, vmem, vmem),
         scratch_shapes=[
@@ -399,7 +412,7 @@
             buffer(2, HALF, VEC, LANES),
             buffer(COLS, 8, LANES),
             buffer(HALF, 8, LANES),
-            buffer(ROW_TILES, 8, LANES),
+            buffer(COL_TILES, 8, LANES),
             buffer(2, COLS, VEC, LANES),
             buffer(2, HALF, VEC, LANES),
             buffer(COLS, VEC, LANES),
@@ -419,10 +432,10 @@
     return pl.pallas_call(
         settle,
         out_shape=shapes,
-        in_specs=[anywhere] * 3,
+        in_specs=[vmem] * 3,
         out_specs=(anywhere, anywhere, anywhere),
         scratch_shapes=[pltpu.SemaphoreType.DMA((3,))],
-    )(*found)
+    )(*[pltpu.with_memory_space_constraint(f, pltpu.VMEM) for f in found])
 
 
 def solution(mesh):

time: 57.8 us -> 53.2 us (0.920)
  Pallas kernels: 56.4 us -> 51.8 us
    pallas_call x2, Pallas kernels: 56.4 us -> 51.8 us  [the longest x1 51.1 us: body(): pl.pallas_call(kernel, out_shape=tuple((pltpu.VMEM(shape.shape, shape.dty...]
where the time goes in v3:
time: 53.2 us; the launch traced here: 53 us
  Pallas kernels  51.8 us (97%)
  between operations  1.29 us (2%)
    pallas_call x1, Pallas kernels, body(): pl.pallas_call(kernel, out_shape=tuple((pltpu.VMEM(shape.shape, shape.dty...  51.1 us

profile of v3, /device:TPU:1, one launch (start us, length us, event | category | flops | bytes accessed | tf_op | source)
XLA Modules:
  0.0 53.0 jit_solution(13883654380564108989)
XLA Ops:
  1.3 51.1 %shard_map.76 = (f32[4,128]{1,0:T(4,128)S(1)}, f32[4,128]{1,0:T(4,128)S(1)}, f32[3,4,4]{2,1,0:T(4,128)S(1)}) custom-call(f32[4,128]{1,0:T(4,128)} %x_hbm.1, f32[8,256,256]{2,1,0:T(8,128)} %tiles_hbm.1, s32[8]{0:T(128)} %rows_hbm.1, s32[8]{0:T(128)} %cols_hbm.1, s32[1]{0:T(128)S(6)} %copy.8.count_hbm), custom_call_target="tpu_custom_call" | custom-call | tf_op jit(solution)/shard_map/pallas_call | solution.py:397
  52.4 0.6 %shard_map.77 = (f32[4,128]{1,0:T(4,128)}, f32[4,128]{1,0:T(4,128)}, f32[3,4,4]{2,1,0:T(4,128)}) custom-call(f32[4,128]{1,0:T(4,128)S(1)} %get-tuple-element.6.basis, f32[4,128]{1,0:T(4,128)S(1)} %get-tuple-element.7.resid, f32[3,4,4]{2,1,0:T(4,128)S(1)} %get-tuple-element.8.coef), custom_call_target="tpu_custom_call" | custom-call | tf_op jit(solution)/shard_map/pallas_call | solution.py:432

commit v4 on v3

--- a/solution.py
+++ b/solution.py
@@ -12,6 +12,9 @@
 HALF = COLS // 2
 ROW_TILES, COL_TILES = 16, 8
 ORDER = ROWS * COLS * LANES
+SPAN, BELOW, WIDE = 8, 3, 1
+KEPT = HALF // (SPAN * WIDE)
+PARTS = SPAN * WIDE
 
 ROW0, COL0, FWD0, BWD0, ROW1, COL1, FWD1, BWD1, PLANE0, LINE0, PLANE1, LINE1, PLANE2, LINE2 = range(14)
 
@@ -111,14 +114,14 @@
 
     turn = lax.rem(x + 4 - 2 * core, 4)
     odd = jnp.where((turn == 1) | (turn == 2), 1, 0)
-    near = lax.rem(z + 9 - y, 8)
-    keeper = near < 4
-    kept_pair = jnp.where(keeper, near, 0) + jnp.where(turn >= 2, 4, 0)
+    near = lax.rem(z + 8 + BELOW - y, 8)
+    keeper = (near < SPAN) & (turn < 2 * WIDE)
+    kept_part = jnp.where(keeper, near + jnp.where(turn >= 2, SPAN, 0), 0)
     kept_group = 2 * r + odd
 
     def keeper_col(g, q):
-        at_z = lax.rem(lax.div(g, 4) + 7 + lax.rem(q, 4), 8)
-        at_x = lax.rem(g + 4 + (2 * lax.rem(g, 2) - 1) * lax.div(q, 4), 4)
+        at_z = lax.rem(lax.div(g, 4) + 8 - BELOW + lax.rem(q, SPAN), 8)
+        at_x = lax.rem(g + 4 + (2 * lax.rem(g, 2) - 1) * lax.div(q, SPAN), 4)
         return 4 * at_z + at_x
 
     def send(src, dst, exchange, row, col):
@@ -150,10 +153,10 @@
     def outward(j, size):
         return size // 2 + lax.div(j + 1, 2) * (1 - 2 * lax.rem(j, 2))
 
-    def over_plane(body):
+    def over_plane(body, first=0, last=COLS - 1):
         def one(j):
             body(4 * lax.rem(z + outward(lax.div(j, 4), 8), 8) + lax.rem(x + outward(lax.rem(j, 4), 4), 4))
-        loop(0, COLS - 1, one)
+        loop(first, last, one)
 
     def over_line(body, count=ROWS - 1):
         def one(j):
@@ -269,29 +272,30 @@
     spread(0, backward, col_at, bp, COL_TILES)
 
     def to_keeper(j):
-        send_or_keep(bp.at[0, pl.ds(14 - 2 * j, 2)], bm.at[r], BWD0, owner_row, keeper_col(c, 7 - j))
-
-    loop(0, 8, to_keeper)
+        q = PARTS - 1 - j
+        send_or_keep(bp.at[0, pl.ds(KEPT * q, KEPT)], bm.at[r], BWD0, owner_row, keeper_col(c, q))
+
+    loop(0, PARTS, to_keeper)
     wait(rsem.at[COL0], xc.at[0])
     for t in range(COL_TILES):
         left, right = twice(xc[0, 2 * t]), twice(xc[0, 2 * t + 1])
         col_parts[2 * t] = split(left, eight)
         col_parts[2 * t + 1] = split(right, eight)
         col_packed[t] = jnp.where(eight < VEC, left, right)
-    line_start(0, crossed(backward, col_at) + start_row, LINE0)
     forward = [multiply(k, col_parts, col_at[k], ((1,), (1,)), masks[k]) for k in range(SLOTS)]
     spread(0, forward, row_at, fp, ROW_TILES)
-    loop(0, HALF, lambda q: send_or_keep(
-        fp.at[0, pl.ds(2 * q, 2)], fm.at[c], FWD0, r, keeper_col(2 * r + lax.div(q, 8), lax.rem(q, 8))))
-    pending.append((BWD0, bp.at[0, pl.ds(0, HALF - 2)], None))
-    pending.append((BWD0, bp.at[0, pl.ds(0, 2)], jnp.logical_not(keeper & (kept_group == c))))
-    pending.append((FWD0, fp.at[0, pl.ds(0, COLS - 2)], None))
-    pending.append((FWD0, fp.at[0, pl.ds(0, 2)], jnp.logical_not(keeper)))
+    loop(0, 2 * PARTS, lambda q: send_or_keep(
+        fp.at[0, pl.ds(KEPT * q, KEPT)], fm.at[c], FWD0, r, keeper_col(2 * r + lax.div(q, PARTS), lax.rem(q, PARTS))))
+    line_start(0, crossed(backward, col_at) + start_row, LINE0)
+    pending.append((BWD0, bp.at[0, pl.ds(0, HALF - KEPT)], None))
+    pending.append((BWD0, bp.at[0, pl.ds(0, KEPT)], jnp.logical_not(keeper & (kept_group == c))))
+    pending.append((FWD0, fp.at[0, pl.ds(0, COLS - KEPT)], None))
+    pending.append((FWD0, fp.at[0, pl.ds(0, KEPT)], jnp.logical_not(keeper)))
     plane_start(0, LINE0, PLANE0)
 
-    kept_at = HALF * odd + 2 * kept_pair
-    at_row = xr.at[1, pl.ds(kept_at, 2)]
-    at_col = xc.at[1, pl.ds(2 * kept_pair, 2)]
+    kept_at = HALF * odd + KEPT * kept_part
+    at_row = xr.at[1, pl.ds(kept_at, KEPT)]
+    at_col = xc.at[1, pl.ds(KEPT * kept_part, KEPT)]
 
     @pl.when(keeper)
     def _():
@@ -299,15 +303,14 @@
         total = jnp.sum(fm[...], axis=0)
         wait(rsem.at[BWD0], bm)
         own[...] = total + jnp.sum(bm[...], axis=0)
+        over_plane(lambda col: send(own, at_row, ROW1, r, col))
         over_line(lambda row: send_or_keep(own, at_col, COL1, row, kept_group), ROWS)
-        over_plane(lambda col: send(own, at_row, ROW1, r, col))
         pltpu.make_async_copy(own, at_row, rsem.at[ROW1]).start()
 
-    for lap in range(2):
+    for lap in range(KEPT):
         pending.append((ROW1, xr.at[1, pl.ds(0, COLS - 1)], keeper))
-    pending.append((COL1, xc.at[1, pl.ds(0, HALF)], keeper))
-    pending.append((COL1, xc.at[1, pl.ds(0, HALF - 2)], keeper))
-    pending.append((COL1, xc.at[1, pl.ds(0, 2)], keeper & (kept_group != c)))
+        pending.append((COL1, xc.at[1, pl.ds(0, ROWS - 1)], keeper))
+    pending.append((COL1, xc.at[1, pl.ds(0, KEPT)], keeper & (kept_group != c)))
 
     gram = plane_done(0, PLANE0)
     _, inverse, inverse_t, _ = factorize(gram, 16)
@@ -324,8 +327,8 @@
             total = total + (of_image[j] * ref[1, at, j : j + 1, :] + of_start[j] * ref[0, at, j : j + 1, :])
         return total
 
-    kept = [apply(inverse, own[at]) + apply(from_start, xr[0, kept_at + at]) for at in range(2)]
-    rest_row = own_gram(kept[0]) + own_gram(kept[1])
+    kept = [apply(inverse, own[at]) + apply(from_start, xr[0, kept_at + at]) for at in range(KEPT)]
+    rest_row = sum(own_gram(block) for block in kept)
     line_start(1, jnp.where(keeper, rest_row, 0.0), LINE1)
     wait(rsem.at[ROW1], xr.at[1])
     for t in range(COLS):
@@ -407,7 +410,7 @@
             buffer(SLOTS, TILE, TILE),
             pltpu.VMEM((SLOTS, TILE, TILE), jnp.bfloat16),
             pltpu.VMEM((SLOTS, TILE, TILE), jnp.bfloat16),
-            buffer(2, VEC, LANES),
+            buffer(KEPT, VEC, LANES),
             buffer(2, COLS, VEC, LANES),
             buffer(2, HALF, VEC, LANES),
             buffer(COLS, 8, LANES),
@@ -417,8 +420,8 @@
             buffer(2, HALF, VEC, LANES),
             buffer(COLS, VEC, LANES),
             buffer(ROWS, VEC, LANES),
-            buffer(COLS, 2, VEC, LANES),
-            buffer(ROWS, 2, VEC, LANES),
+            buffer(COLS, KEPT, VEC, LANES),
+            buffer(ROWS, KEPT, VEC, LANES),
             buffer(6, 1, LANES),
             buffer(3, ROWS, 1, LANES),
             buffer(3, COLS, 1, LANES),

time: 53.2 us -> 51.9 us (0.976)
  Pallas kernels: 51.8 us -> 50.5 us
    pallas_call x1, Pallas kernels: 51.1 us -> 49.9 us  [body(): pl.pallas_call(kernel, out_shape=tuple((pltpu.VMEM(shape.shape, shape.dty...]
where the time goes in v4:
time: 51.9 us; the launch traced here: 51.8 us
  Pallas kernels  50.5 us (97%)
  between operations  1.29 us (2%)
    pallas_call x1, Pallas kernels, body(): pl.pallas_call(kernel, out_shape=tuple((pltpu.VMEM(shape.shape, shape.dty...  49.9 us

profile of v4, /device:TPU:1, one launch (start us, length us, event | category | flops | bytes accessed | tf_op | source)
XLA Modules:
  0.0 51.8 jit_solution(14336000032905606042)
XLA Ops:
  1.3 49.9 %shard_map.76 = (f32[4,128]{1,0:T(4,128)S(1)}, f32[4,128]{1,0:T(4,128)S(1)}, f32[3,4,4]{2,1,0:T(4,128)S(1)}) custom-call(f32[4,128]{1,0:T(4,128)} %x_hbm.1, f32[8,256,256]{2,1,0:T(8,128)} %tiles_hbm.1, s32[8]{0:T(128)} %rows_hbm.1, s32[8]{0:T(128)} %cols_hbm.1, s32[1]{0:T(128)S(6)} %copy.8.count_hbm), custom_call_target="tpu_custom_call" | custom-call | tf_op jit(solution)/shard_map/pallas_call | solution.py:400
  51.2 0.6 %shard_map.77 = (f32[4,128]{1,0:T(4,128)}, f32[4,128]{1,0:T(4,128)}, f32[3,4,4]{2,1,0:T(4,128)}) custom-call(f32[4,128]{1,0:T(4,128)S(1)} %get-tuple-element.6.basis, f32[4,128]{1,0:T(4,128)S(1)} %get-tuple-element.7.resid, f32[3,4,4]{2,1,0:T(4,128)S(1)} %get-tuple-element.8.coef), custom_call_target="tpu_custom_call" | custom-call | tf_op jit(solution)/shard_map/pallas_call | solution.py:435

commit v5 on v4

--- a/solution.py
+++ b/solution.py
@@ -12,9 +12,7 @@
 HALF = COLS // 2
 ROW_TILES, COL_TILES = 16, 8
 ORDER = ROWS * COLS * LANES
-SPAN, BELOW, WIDE = 8, 3, 1
-KEPT = HALF // (SPAN * WIDE)
-PARTS = SPAN * WIDE
+KEPT = 2
 
 ROW0, COL0, FWD0, BWD0, ROW1, COL1, FWD1, BWD1, PLANE0, LINE0, PLANE1, LINE1, PLANE2, LINE2 = range(14)
 
@@ -113,16 +111,10 @@
     eight = iota((8, LANES), 0)
 
     turn = lax.rem(x + 4 - 2 * core, 4)
-    odd = jnp.where((turn == 1) | (turn == 2), 1, 0)
-    near = lax.rem(z + 8 + BELOW - y, 8)
-    keeper = (near < SPAN) & (turn < 2 * WIDE)
-    kept_part = jnp.where(keeper, near + jnp.where(turn >= 2, SPAN, 0), 0)
+    keeper = turn < 2
+    odd = lax.rem(turn, 2)
+    kept_part = lax.rem(z + 8 - y, 8)
     kept_group = 2 * r + odd
-
-    def keeper_col(g, q):
-        at_z = lax.rem(lax.div(g, 4) + 8 - BELOW + lax.rem(q, SPAN), 8)
-        at_x = lax.rem(g + 4 + (2 * lax.rem(g, 2) - 1) * lax.div(q, SPAN), 4)
-        return 4 * at_z + at_x
 
     def send(src, dst, exchange, row, col):
         pltpu.make_async_remote_copy(
@@ -150,18 +142,21 @@
             return carry
         lax.fori_loop(first, last, step, 0)
 
-    def outward(j, size):
-        return size // 2 + lax.div(j + 1, 2) * (1 - 2 * lax.rem(j, 2))
-
-    def over_plane(body, first=0, last=COLS - 1):
-        def one(j):
-            body(4 * lax.rem(z + outward(lax.div(j, 4), 8), 8) + lax.rem(x + outward(lax.rem(j, 4), 4), 4))
-        loop(first, last, one)
+    def outward(size):
+        return [size // 2 + (j + 1) // 2 * (1 - 2 * (j % 2)) for j in range(size)]
+
+    plane_z = [4 * lax.rem(z + away, 8) for away in outward(8)]
+    plane_x = [lax.rem(x + away, 4) for away in outward(4)]
+    line_y = [2 * lax.rem(y + away, 8) for away in outward(8)]
+    line_core = [1 - core, core]
+
+    def over_plane(body):
+        for at in range(COLS - 1):
+            body(plane_z[at // 4] + plane_x[at % 4])
 
     def over_line(body, count=ROWS - 1):
-        def one(j):
-            body(2 * lax.rem(y + outward(lax.div(j, 2), 8), 8) + lax.rem(core + 1 + lax.rem(j, 2), 2))
-        loop(0, count, one)
+        for at in range(count):
+            body(line_y[at // 2] + line_core[at % 2])
 
     pending = []
 
@@ -175,7 +170,8 @@
 
     @pl.when(owner_row != r)
     def _():
-        loop(0, HALF, lambda j: greet(owner_row, owner_col + j))
+        for j in range(HALF):
+            greet(owner_row, owner_col + j)
 
     over_plane(lambda col: greet(r, col))
     for k in range(SLOTS):
@@ -271,11 +267,8 @@
     backward = [multiply(k, row_parts, row_at[k], ((1,), (0,)), masks[k]) for k in range(SLOTS)]
     spread(0, backward, col_at, bp, COL_TILES)
 
-    def to_keeper(j):
-        q = PARTS - 1 - j
-        send_or_keep(bp.at[0, pl.ds(KEPT * q, KEPT)], bm.at[r], BWD0, owner_row, keeper_col(c, q))
-
-    loop(0, PARTS, to_keeper)
+    for at, q in enumerate(outward(8)):
+        send_or_keep(bp.at[0, pl.ds(KEPT * q, KEPT)], bm.at[r], BWD0, owner_row, plane_z[at] + x)
     wait(rsem.at[COL0], xc.at[0])
     for t in range(COL_TILES):
         left, right = twice(xc[0, 2 * t]), twice(xc[0, 2 * t + 1])
@@ -284,8 +277,11 @@
         col_packed[t] = jnp.where(eight < VEC, left, right)
     forward = [multiply(k, col_parts, col_at[k], ((1,), (1,)), masks[k]) for k in range(SLOTS)]
     spread(0, forward, row_at, fp, ROW_TILES)
-    loop(0, 2 * PARTS, lambda q: send_or_keep(
-        fp.at[0, pl.ds(KEPT * q, KEPT)], fm.at[c], FWD0, r, keeper_col(2 * r + lax.div(q, PARTS), lax.rem(q, PARTS))))
+    for at, away in enumerate(outward(8)):
+        q = lax.rem(z + 8 - y + away, 8)
+        for half in range(2):
+            part = fp.at[0, pl.ds(HALF * half + KEPT * q, KEPT)]
+            send_or_keep(part, fm.at[c], FWD0, r, plane_z[at] + 2 * core + half)
     line_start(0, crossed(backward, col_at) + start_row, LINE0)
     pending.append((BWD0, bp.at[0, pl.ds(0, HALF - KEPT)], None))
     pending.append((BWD0, bp.at[0, pl.ds(0, KEPT)], jnp.logical_not(keeper & (kept_group == c))))
@@ -340,7 +336,8 @@
         s = lax.rem(c + j, HALF)
         send_or_keep(bp.at[1, s], br.at[r], BWD1, owner_row, owner_col + s)
 
-    loop(0, HALF, back)
+    for j in range(HALF):
+        back(j)
     wait(rsem.at[COL1], xc.at[1])
     for t in range(COL_TILES):
         left, right = combined(xc, 2 * t), combined(xc, 2 * t + 1)

time: 51.9 us -> 51.4 us (level)
  no operation moved by 1% of the time
where the time goes in v5:
time: 51.4 us; the launch traced here: 51.3 us
  Pallas kernels  50 us (97%)
  between operations  1.29 us (3%)
    pallas_call x1, Pallas kernels, body(): pl.pallas_call(kernel, out_shape=tuple((pltpu.VMEM(shape.shape, shape.dty...  49.4 us

profile of v5, /device:TPU:1, one launch (start us, length us, event | category | flops | bytes accessed | tf_op | source)
XLA Modules:
  0.0 51.3 jit_solution(15541321477773568928)
XLA Ops:
  1.3 49.4 %shard_map.76 = (f32[4,128]{1,0:T(4,128)S(1)}, f32[4,128]{1,0:T(4,128)S(1)}, f32[3,4,4]{2,1,0:T(4,128)S(1)}) custom-call(f32[4,128]{1,0:T(4,128)} %x_hbm.1, f32[8,256,256]{2,1,0:T(8,128)} %tiles_hbm.1, s32[8]{0:T(128)} %rows_hbm.1, s32[8]{0:T(128)} %cols_hbm.1, s32[1]{0:T(128)S(6)} %copy.8.count_hbm), custom_call_target="tpu_custom_call" | custom-call | tf_op jit(solution)/shard_map/pallas_call | solution.py:397
  50.7 0.6 %shard_map.77 = (f32[4,128]{1,0:T(4,128)}, f32[4,128]{1,0:T(4,128)}, f32[3,4,4]{2,1,0:T(4,128)}) custom-call(f32[4,128]{1,0:T(4,128)S(1)} %get-tuple-element.6.basis, f32[4,128]{1,0:T(4,128)S(1)} %get-tuple-element.7.resid, f32[3,4,4]{2,1,0:T(4,128)S(1)} %get-tuple-element.8.coef), custom_call_target="tpu_custom_call" | custom-call | tf_op jit(solution)/shard_map/pallas_call | solution.py:432

commit v6 on v5

--- a/solution.py
+++ b/solution.py
@@ -166,13 +166,13 @@
     def greet(row, col):
         pl.semaphore_signal(barrier, 1, device_id=(row, col), device_id_type=MESH)
 
-    over_line(lambda row: greet(row, group))
 
     @pl.when(owner_row != r)
     def _():
         for j in range(HALF):
             greet(owner_row, owner_col + j)
 
+    over_line(lambda row: greet(row, group))
     over_plane(lambda col: greet(r, col))
     for k in range(SLOTS):
         pltpu.make_async_copy(tiles_hbm.at[k], raw.at[k], tsem.at[k]).start()
@@ -336,8 +336,6 @@
         s = lax.rem(c + j, HALF)
         send_or_keep(bp.at[1, s], br.at[r], BWD1, owner_row, owner_col + s)
 
-    for j in range(HALF):
-        back(j)
     wait(rsem.at[COL1], xc.at[1])
     for t in range(COL_TILES):
         left, right = combined(xc, 2 * t), combined(xc, 2 * t + 1)
@@ -345,6 +343,8 @@
         col_parts[2 * t + 1] = split(right, eight)
         col_packed[t] = jnp.where(eight < VEC, left, right)
     line_start(2, crossed(backward, col_at), LINE2)
+    for j in range(HALF):
+        back(j)
     forward = [multiply(k, col_parts, col_at[k], ((1,), (1,)), masks[k]) for k in range(SLOTS)]
     spread(1, forward, row_at, fp, ROW_TILES)
     over_plane(lambda col: send(fp.at[1, col], fr.at[c], FWD1, r, col))

time: 51.4 us -> 51.1 us (level)
  no operation moved by 1% of the time
where the time goes in v6:
time: 51.1 us; the launch traced here: 50.9 us
  Pallas kernels  49.7 us (97%)
  between operations  1.29 us (3%)
    pallas_call x1, Pallas kernels, body(): pl.pallas_call(kernel, out_shape=tuple((pltpu.VMEM(shape.shape, shape.dty...  49 us

profile of v6, /device:TPU:1, one launch (start us, length us, event | category | flops | bytes accessed | tf_op | source)
XLA Modules:
  0.0 50.9 jit_solution(3720232911995345853)
XLA Ops:
  1.3 49.0 %shard_map.76 = (f32[4,128]{1,0:T(4,128)S(1)}, f32[4,128]{1,0:T(4,128)S(1)}, f32[3,4,4]{2,1,0:T(4,128)S(1)}) custom-call(f32[4,128]{1,0:T(4,128)} %x_hbm.1, f32[8,256,256]{2,1,0:T(8,128)} %tiles_hbm.1, s32[8]{0:T(128)} %rows_hbm.1, s32[8]{0:T(128)} %cols_hbm.1, s32[1]{0:T(128)S(6)} %copy.8.count_hbm), custom_call_target="tpu_custom_call" | custom-call | tf_op jit(solution)/shard_map/pallas_call | solution.py:397
  50.3 0.6 %shard_map.77 = (f32[4,128]{1,0:T(4,128)}, f32[4,128]{1,0:T(4,128)}, f32[3,4,4]{2,1,0:T(4,128)}) custom-call(f32[4,128]{1,0:T(4,128)S(1)} %get-tuple-element.6.basis, f32[4,128]{1,0:T(4,128)S(1)} %get-tuple-element.7.resid, f32[3,4,4]{2,1,0:T(4,128)S(1)} %get-tuple-element.8.coef), custom_call_target="tpu_custom_call" | custom-call | tf_op jit(solution)/shard_map/pallas_call | solution.py:432
